TPU v7x, 512 devices: a whole 4x4x16 slice. The times are simulated.
512 devices in a mesh: shot: 16 (over z_hi, y), slab: 32 (over z_lo, x, core).
Axes of the slice: x: 4, y: 4, z: 16 (z_hi: 4, z_lo: 4; z = z_hi * 4 + z_lo), core: 2. Of those that a mesh axis runs over, the one named last changes fastest.
Arguments:
- wave_now: float32 [16, 512, 64, 128], P('shot', 'slab'), may hold values from -6 to 6
- wave_prev: float32 [16, 512, 64, 128], P('shot', 'slab'), may hold values from -6 to 6
- courant: float32 [512, 64, 128], P('slab'), may hold values from 0.05 to 0.2
- forward: bfloat16 [16, 3, 512, 64, 128], P('shot', None, 'slab'), may hold values from -6 to 6
- receivers: int32 [16, 3, 256], P('shot'), may hold values from 0 to 511, as said below
- residual: float32 [16, 3, 256], P('shot'), may hold values from -6 to 6
- aperture: int32 [16, 2], P('shot'), may hold values from 0 to 512, as said below
- latent: bfloat16 [256, 32, 4096], P('slab', 'shot')
- weight: float32 [64, 8], replicated, may hold values from -0.75 to 0.75
Outputs:
- wave_after: float32 [16, 512, 64, 128], P('shot', 'slab')
- wave_before: float32 [16, 512, 64, 128], P('shot', 'slab')
- latent_grad: float32 [256, 32, 4096], P('slab', 'shot')
- weight_grad: float32 [64, 8], replicated
Inputs may be any that keep to these rules, and one draw needn't show every extreme that they name: receivers[s,0,r], receivers[s,1,r], receivers[s,2,r] are an x, y and depth cell inside the grid. Each shot's aperture is a range of at least 512 // 4 x cells with aperture[s,0] < aperture[s,1].
All inputs are finite; a program needn't handle non-finite values.
Results may differ from a plain program's by a relative error of at most 0.0003.
Values sent between devices are 32-bit elements; how exact they have to be, the bound alone decides.
No kernel may reach another device: no remote copies, remote signals or barrier semaphores. Data moves between devices by JAX's collectives and lax.ppermute only.
A program may use at most 64 MiB of HBM per device.

v0:
```python
import math
import jax
import jax.numpy as jnp
from jax import lax
from jax.sharding import PartitionSpec as P

STEPS = 3
stencil_weights = (-205.0 / 72.0, 8.0 / 5.0, -1.0 / 5.0, 8.0 / 315.0, -1.0 / 560.0)


def extended(block, sides, width):
    for axis, dim in sides:
        count = lax.axis_size(axis)
        forward = [(i, i + 1) for i in range(count - 1)]
        backward = [(target, source) for source, target in forward]
        low = lax.ppermute(
            lax.slice_in_dim(block, block.shape[dim] - width, None, axis=dim), axis, forward
        )
        high = lax.ppermute(lax.slice_in_dim(block, 0, width, axis=dim), axis, backward)
        block = jnp.concatenate([low, block, high], axis=dim)
    return block


def laplace(padded):
    size_x = padded.shape[0] - 8
    size_y = padded.shape[1] - 8
    size_z = padded.shape[2] - 8

    def moved(shift_x, shift_y, shift_z):
        return padded[
            4 + shift_x : 4 + shift_x + size_x,
            4 + shift_y : 4 + shift_y + size_y,
            4 + shift_z : 4 + shift_z + size_z,
        ]

    total = 3.0 * stencil_weights[0] * moved(0, 0, 0)
    for offset in range(1, 5):
        cycle_sum = moved(offset, 0, 0) + moved(-offset, 0, 0)
        cycle_sum = cycle_sum + moved(0, offset, 0) + moved(0, -offset, 0)
        cycle_sum = cycle_sum + moved(0, 0, offset) + moved(0, 0, -offset)
        total = total + stencil_weights[offset] * cycle_sum
    return total


def pad_sides(field):
    return jnp.pad(field, ((0, 0), (4, 4), (4, 4)))


def inject(field, receivers, values, first_x):
    extent = field.shape[0]
    local_x = receivers[0, 0] - first_x
    valid = (local_x >= 0) & (local_x < extent)
    local_x = jnp.where(valid, local_x, extent)
    return field.at[local_x, receivers[0, 1], receivers[0, 2]].add(values, mode="drop")


def body(wave_now, wave_prev, courant, forward, receivers, residual, aperture, latent, weight):
    slab_cells = courant.shape[0]
    first_x = lax.axis_index("slab") * slab_cells
    current = wave_now[0]
    previous = wave_prev[0]
    accum = jnp.zeros(current.shape, jnp.float32)
    for instant in range(STEPS):
        padded = extended(current, (("slab", 0),), 4)
        advanced = 2.0 * current - previous + courant * laplace(pad_sides(padded))
        advanced = inject(advanced, receivers, residual[0, instant], first_x)
        accum = accum + advanced * forward[0, instant].astype(jnp.float32)
        previous = current
        current = advanced
    x_cells = first_x + jnp.arange(slab_cells, dtype=jnp.int32)
    inside = (x_cells >= aperture[0, 0]) & (x_cells < aperture[0, 1])
    image = jnp.where(inside[:, None, None], courant * accum, 0.0)
    image_rows = image.transpose(1, 0, 2)
    tile_rows = image_rows.shape[0] // lax.axis_size("shot")
    tile = lax.psum_scatter(image_rows, "shot", scatter_dimension=0, tiled=True).transpose(1, 0, 2)
    half_x = slab_cells // 2
    half_y = tile_rows // 2
    half_z = tile.shape[2] // 2
    taps = (
        tile.reshape(half_x, 2, half_y, 2, half_z, 2)
        .transpose(0, 2, 4, 1, 3, 5)
        .reshape(half_x, half_y, half_z, 8)
    )
    channels = weight.shape[0]
    latent_grad = jnp.einsum(
        "ijkq,cq->ijck", taps, weight, precision=lax.Precision.HIGHEST
    ).reshape(half_x, half_y, channels * half_z)
    latent_wide = latent.astype(jnp.float32).reshape(half_x, half_y, channels, half_z)
    partial_grad = jnp.einsum("ijck,ijkq->cq", latent_wide, taps, precision=lax.Precision.HIGHEST)
    latent_cells = (
        latent.shape[0] * lax.axis_size("slab") * latent.shape[1] * lax.axis_size("shot") * half_z
    )
    weight_grad = lax.psum(partial_grad, ("shot", "slab")) * (1.0 / math.sqrt(latent_cells))
    return (current[None], previous[None], latent_grad, weight_grad)


def solution(mesh):
    return jax.shard_map(
        body,
        mesh=mesh,
        in_specs=(
            P("shot", "slab", None, None),
            P("shot", "slab", None, None),
            P("slab", None, None),
            P("shot", None, "slab", None, None),
            P("shot", None, None),
            P("shot", None, None),
            P("shot", None),
            P("slab", "shot", None),
            P(),
        ),
        out_specs=(
            P("shot", "slab", None, None),
            P("shot", "slab", None, None),
            P("slab", "shot", None),
            P(),
        ),
        check_vma=False,
    )
```

profile of v0, /device:TPU:1, one launch (start us, length us, event | category | flops | bytes accessed | tf_op | source)
XLA Modules:
  0.0 334.7 jit_solution(5647150959445888792)
XLA Ops:
  7.2 0.0 copy-start
  7.2 0.0 copy-start.4
  7.2 0.0 copy-start.3
  7.2 0.0 reduce-scatter.2.cloned.1.call-start
  7.2 1.1 slice_bitcast_fusion.1
  8.3 8.8 %collective-permute-start = (f32[4,64,128]{2,1,0:T(8,128)S(1)}, f32[4,64,128]{2,1,0:T(8,128)S(1)}, u32[]{:S(2)}, u32[]{:S(2)}) collective-permute-start(f32[4,64,128]{2,1,0:T(8,128)S(1)} %get-tuple-element.24), channel_id=1, source_target_pairs={{1,0},{2,1},{3,2},{4,3},{5,4},{6,5},{7,6},{8,7},{9,8},{10,9},{11,1... | collective-permute-start | bytes 393224 | tf_op jit(solution)/shard_map/ppermute | solution.py:19
  17.1 1.9 collective-permute-start.1
  19.0 0.7 fusion.67
  19.8 0.7 or_select_fusion
  20.5 0.0 collective-permute-done
  20.5 0.5 collective-permute-done.1
  21.0 0.0 copy-start.6
  21.0 0.7 copy-done.6
  21.6 1.6 select_maximum_fusion.4
  23.2 0.0 copy-done.4
  23.2 0.0 copy-done.3
  23.2 3.7 %fusion.13 = f32[16,64,128]{2,1,0:T(8,128)S(1)} fusion(f32[16,64,128]{2,1,0:T(8,128)S(1)} %copy-done.3, f32[16,64,128]{2,1,0:T(8,128)S(1)} %bitcast.63, f32[4,64,128]{2,1,0:T(8,128)} %copy-done.6, f32[4,64,128]{2,1,0:T(8,128)S(1)} %collective-permute-done, f32[24,72,136]{2,1,0:T(8,128)S(1)} %select_maximum_fusion.4, f32[1,16,64,128]{3,2,1,0:T(8,128)} %param.10), kind=kLoop, calls=%fused_computation.40 | loop fusion | flops 5373952 | bytes 10747904 | tf_op jit(solution)/shard_map/add | solution.py:65
  26.9 15.6 %scatter_fusion = f32[16,64,128]{2,1,0:T(8,128)S(1)} fusion(f32[16,64,128]{2,1,0:T(8,128)S(1)} %fusion.13, s32[256]{0:T(256)S(1)} %bitcast.56, f32[256]{0:T(256)S(1)} %bitcast.69), kind=kCustom, calls=%fused_computation | custom fusion | flops 256 | bytes 6144 | tf_op jit(solution)/shard_map/scatter-add | solution.py:54
  42.5 4.3 %collective-permute-start.3 = (f32[4,64,128]{2,1,0:T(8,128)S(1)}, f32[4,64,128]{2,1,0:T(8,128)S(1)}, u32[]{:S(2)}, u32[]{:S(2)}) collective-permute-start(f32[4,64,128]{2,1,0:T(8,128)S(1)} %get-tuple-element.22), channel_id=1, source_target_pairs={{0,1},{1,2},{2,3},{3,4},{4,5},{5,6},{6,7},{7,8},{8,9},{9,10},{10,1... | collective-permute-start | bytes 393224 | tf_op jit(solution)/shard_map/ppermute | solution.py:16
  46.8 1.9 collective-permute-start.2
  48.8 0.0 collective-permute-done.3
  48.8 0.1 constant_dynamic-update-slice_fusion.1
  48.9 4.2 %collective-permute-done.2 = f32[4,64,128]{2,1,0:T(8,128)S(1)} collective-permute-done((f32[4,64,128]{2,1,0:T(8,128)S(1)}, f32[4,64,128]{2,1,0:T(8,128)S(1)}, u32[]{:S(2)}, u32[]{:S(2)}) %collective-permute-start.2) | collective-permute-done | bytes 131104 | tf_op jit(solution)/shard_map/ppermute | solution.py:19
  53.1 0.5 select_maximum_fusion.2
  53.7 2.1 fusion.46
  55.8 0.0 copy-start.8
  55.8 15.6 %scatter_fusion.1 = f32[16,64,128]{2,1,0:T(8,128)S(1)} fusion(f32[16,64,128]{2,1,0:T(8,128)S(1)} %fusion.46, s32[256]{0:T(256)S(1)} %bitcast.57, f32[256]{0:T(256)S(1)} %bitcast.68), kind=kCustom, calls=%fused_computation.1 | custom fusion | flops 256 | bytes 6144 | tf_op jit(solution)/shard_map/scatter-add | solution.py:54
  71.4 0.0 copy-start.1
  71.4 1.9 collective-permute-start.5
  73.3 0.0 copy-done.8
  73.3 0.6 fusion.68
  73.9 1.3 compare_and_fusion
  75.2 2.6 collective-permute-start.4
  77.8 0.0 collective-permute-done.5
  77.8 0.1 constant_dynamic-update-slice_fusion.5
  78.0 3.5 %collective-permute-done.4 = f32[4,64,128]{2,1,0:T(8,128)S(1)} collective-permute-done((f32[4,64,128]{2,1,0:T(8,128)S(1)}, f32[4,64,128]{2,1,0:T(8,128)S(1)}, u32[]{:S(2)}, u32[]{:S(2)}) %collective-permute-start.4) | collective-permute-done | bytes 131104 | tf_op jit(solution)/shard_map/ppermute | solution.py:19
  81.5 0.5 select_maximum_fusion
  82.1 2.1 fusion.36
  84.2 0.0 copy-start.5
  84.2 15.6 %scatter_fusion.2 = f32[16,64,128]{2,1,0:T(8,128)S(1)} fusion(f32[16,64,128]{2,1,0:T(8,128)S(1)} %fusion.36, s32[256]{0:T(256)S(1)} %bitcast.58, f32[256]{0:T(256)S(1)} %bitcast.67), kind=kCustom, calls=%fused_computation.2 | custom fusion | flops 256 | bytes 6144 | tf_op jit(solution)/shard_map/scatter-add | solution.py:54
  99.7 0.0 copy-done.1
  99.7 0.0 copy-done.5
  99.8 0.0 copy-start.2
  99.8 0.0 copy-start.7
  99.8 0.3 fusion.58
  100.1 1.1 copy.23
  101.2 0.0 copy-done.2
  101.2 0.0 reduce-scatter.2.cloned.1.call-update
  101.2 0.0 copy-done.7
  101.2 0.2 reshape.127
  101.4 118.1 %reduce-scatter.2.cloned.1.call-done = f32[4,16,128]{2,1,0:T(8,128)} async-done(((f32[64,16,128]{2,1,0:T(8,128)}), f32[4,16,128]{2,1,0:T(8,128)}) %reduce-scatter.2.cloned.1.call-update) | async-done | bytes 32784 | tf_op jit(solution)/shard_map/reduce_scatter | solution.py:75
  219.6 2.8 reshape.124
  222.4 0.7 copy.24
  223.1 0.0 copy-done
  223.1 1.0 convolution_bitcast_fusion
  224.1 0.2 copy.31
  224.3 1.0 reshape.151
  225.3 0.3 convolution_bitcast_fusion.1
  225.6 101.6 %psum.7 = f32[64,8]{0,1:T(8,128)S(1)} all-reduce(f32[64,8]{0,1:T(8,128)S(1)} %convolution_bitcast_fusion.1), channel_id=1, replica_groups=mesh['shot'=16,'slab'=32] {'shot','slab'}, use_global_device_ids=true, to_apply=%region_4.5 | all-reduce | flops 512 | bytes 4096 | tf_op jit(solution)/shard_map/psum | solution.py:93
  327.2 0.6 broadcast_multiply_fusion
  (6 shorter events, 0.1 us)
Async XLA Ops:
  7.2 215.9 %copy-start = (f32[64,8]{0,1:T(8,128)S(1)}, f32[64,8]{0,1:T(8,128)}, u32[]{:S(2)}) copy-start(f32[64,8]{0,1:T(8,128)} %param.17) | copy-start | bytes 6148
  7.2 16.0 %copy-start.4 = (f32[1,16,64,128]{3,2,1,0:T(8,128)S(1)}, f32[1,16,64,128]{3,2,1,0:T(8,128)}, u32[]{:S(2)}) copy-start(f32[1,16,64,128]{3,2,1,0:T(8,128)} %param.9) | copy-start | bytes 1572868
  7.2 16.0 %copy-start.3 = (f32[16,64,128]{2,1,0:T(8,128)S(1)}, f32[16,64,128]{2,1,0:T(8,128)}, u32[]{:S(2)}) copy-start(f32[16,64,128]{2,1,0:T(8,128)} %param.11) | copy-start | bytes 1572868
  7.2 212.3 %reduce-scatter.2.cloned.1.call-start = ((), (), s32[]{:S(2)}) async-start(), calls=%async_computation.1 | async-start | bytes 557056 | tf_op jit(solution)/shard_map/reduce_scatter | solution.py:75
  8.3 12.2 %collective-permute-start = (f32[4,64,128]{2,1,0:T(8,128)S(1)}, f32[4,64,128]{2,1,0:T(8,128)S(1)}, u32[]{:S(2)}, u32[]{:S(2)}) collective-permute-start(f32[4,64,128]{2,1,0:T(8,128)S(1)} %get-tuple-element.24), channel_id=1, source_target_pairs={{1,0},{2,1},{3,2},{4,3},{5,4},{6,5},{7,6},{8,7},{9,8},{10,9},{11,1... | collective-permute-start | bytes 393224 | tf_op jit(solution)/shard_map/ppermute | solution.py:19
  17.1 3.9 %collective-permute-start.1 = (f32[4,64,128]{2,1,0:T(8,128)S(1)}, f32[4,64,128]{2,1,0:T(8,128)S(1)}, u32[]{:S(2)}, u32[]{:S(2)}) collective-permute-start(f32[4,64,128]{2,1,0:T(8,128)S(1)} %get-tuple-element.25), channel_id=1, source_target_pairs={{0,1},{1,2},{2,3},{3,4},{4,5},{5,6},{6,7},{7,8},{8,9},{9,10},{10,1... | collective-permute-start | bytes 393224 | tf_op jit(solution)/shard_map/ppermute | solution.py:16
  21.0 0.7 copy-start.6
  42.5 6.3 %collective-permute-start.3 = (f32[4,64,128]{2,1,0:T(8,128)S(1)}, f32[4,64,128]{2,1,0:T(8,128)S(1)}, u32[]{:S(2)}, u32[]{:S(2)}) collective-permute-start(f32[4,64,128]{2,1,0:T(8,128)S(1)} %get-tuple-element.22), channel_id=1, source_target_pairs={{0,1},{1,2},{2,3},{3,4},{4,5},{5,6},{6,7},{7,8},{8,9},{9,10},{10,1... | collective-permute-start | bytes 393224 | tf_op jit(solution)/shard_map/ppermute | solution.py:16
  46.8 6.3 %collective-permute-start.2 = (f32[4,64,128]{2,1,0:T(8,128)S(1)}, f32[4,64,128]{2,1,0:T(8,128)S(1)}, u32[]{:S(2)}, u32[]{:S(2)}) collective-permute-start(f32[4,64,128]{2,1,0:T(8,128)S(1)} %get-tuple-element.23), channel_id=1, source_target_pairs={{1,0},{2,1},{3,2},{4,3},{5,4},{6,5},{7,6},{8,7},{9,8},{10,9},{11,1... | collective-permute-start | bytes 393224 | tf_op jit(solution)/shard_map/ppermute | solution.py:19
  55.8 17.5 %copy-start.8 = (s32[1,2]{1,0:T(1,128)S(1)}, s32[1,2]{1,0:T(1,128)}, u32[]{:S(2)}) copy-start(s32[1,2]{1,0:T(1,128)} %param.15) | copy-start | bytes 28
  71.4 28.4 %copy-start.1 = (f32[16,64,128]{2,1,0:T(8,128)}, f32[16,64,128]{2,1,0:T(8,128)S(1)}, u32[]{:S(2)}) copy-start(f32[16,64,128]{2,1,0:T(8,128)S(1)} %scatter_fusion.1) | copy-start | bytes 1572868
  71.4 6.4 %collective-permute-start.5 = (f32[4,64,128]{2,1,0:T(8,128)S(1)}, f32[4,64,128]{2,1,0:T(8,128)S(1)}, u32[]{:S(2)}, u32[]{:S(2)}) collective-permute-start(f32[4,64,128]{2,1,0:T(8,128)S(1)} %get-tuple-element.18), channel_id=1, source_target_pairs={{0,1},{1,2},{2,3},{3,4},{4,5},{5,6},{6,7},{7,8},{8,9},{9,10},{10,1... | collective-permute-start | bytes 393224 | tf_op jit(solution)/shard_map/ppermute | solution.py:16
  75.2 6.3 %collective-permute-start.4 = (f32[4,64,128]{2,1,0:T(8,128)S(1)}, f32[4,64,128]{2,1,0:T(8,128)S(1)}, u32[]{:S(2)}, u32[]{:S(2)}) collective-permute-start(f32[4,64,128]{2,1,0:T(8,128)S(1)} %get-tuple-element.19), channel_id=1, source_target_pairs={{1,0},{2,1},{3,2},{4,3},{5,4},{6,5},{7,6},{8,7},{9,8},{10,9},{11,1... | collective-permute-start | bytes 393224 | tf_op jit(solution)/shard_map/ppermute | solution.py:19
  84.2 15.6 %copy-start.5 = (bf16[1,3,16,64,128]{4,3,2,1,0:T(8,128)(2,1)S(1)}, bf16[1,3,16,64,128]{4,3,2,1,0:T(8,128)(2,1)}, u32[]{:S(2)}) copy-start(bf16[1,3,16,64,128]{4,3,2,1,0:T(8,128)(2,1)} %param.12) | copy-start | bytes 2359300
  99.8 1.4 copy-start.2
  99.8 1.4 copy-start.7
Sparse Core Ops, SparseCore 0:
  101.3 118.1 reduce-scatter.1
where the time goes:
time: 335 us
  waiting for transfers between devices  126 us (38%)
  blocking collectives  102 us (30%)
  other arithmetic  60 us (18%)
  starting transfers between devices  21.5 us (6%)
  between operations  14.4 us (4%)
  local copies, waits for them, and re-layouts  9.37 us (3%)
    reduce_scatter x1, waiting for transfers between devices, body(): lax.psum_scatter(image_rows, 'shot', scatter_dimension=0, tiled=True)  118 us
    psum x1, blocking collectives, body(): lax.psum(partial_grad, ('shot', 'slab')) * (1.0 / math.sqrt(latent_cells))  102 us
    scatter-add x3, other arithmetic, inject(): field.at[local_x, receivers[0, 1], receivers[0, 2]].add(values, mode='drop')  46.7 us
    ppermute x3, starting transfers between devices, extended(): lax.ppermute(lax.slice_in_dim(block, 0, width, axis=dim), axis, backward)  13.3 us
    ppermute x3, starting transfers between devices, extended(): lax.ppermute(lax.slice_in_dim(block, block.shape[dim] - width, None, axis...  8.19 us
    add x3, other arithmetic, body(): advanced = 2.0 * current - previous + courant * laplace(pad_sides(padded))  7.87 us
    ppermute x3, waiting for transfers between devices, extended(): lax.ppermute(lax.slice_in_dim(block, 0, width, axis=dim), axis, backward)  7.76 us
  transfers between devices with their start and end apart: 7, of which 4 were waited for; matrix products, arithmetic and copies ran while one was open for 1% of the time, Pallas kernels for 0%

commit v1 on v0

--- a/solution.py
+++ b/solution.py
@@ -90,7 +90,7 @@
     latent_cells = (
         latent.shape[0] * lax.axis_size("slab") * latent.shape[1] * lax.axis_size("shot") * half_z
     )
-    weight_grad = lax.psum(partial_grad, ("shot", "slab")) * (1.0 / math.sqrt(latent_cells))
+    weight_grad = lax.psum(lax.psum(partial_grad, "shot"), "slab") * (1.0 / math.sqrt(latent_cells))
     return (current[None], previous[None], latent_grad, weight_grad)
 
 

time: 335 us -> 355 us (1.060)
  blocking collectives: 102 us -> 121 us
    psum x1 -> x2, blocking collectives: 102 us -> 121 us  [the longest x1 76.7 us: body(): lax.psum(lax.psum(partial_grad, 'shot'), 'slab')]
where the time goes in v1:
time: 355 us
  waiting for transfers between devices  126 us (35%)
  blocking collectives  121 us (34%)
  other arithmetic  61.4 us (17%)
  starting transfers between devices  21.6 us (6%)
  between operations  14.4 us (4%)
  local copies, waits for them, and re-layouts  8.71 us (2%)
    reduce_scatter x1, waiting for transfers between devices, body(): lax.psum_scatter(image_rows, 'shot', scatter_dimension=0, tiled=True)  118 us
    psum x1, blocking collectives, body(): lax.psum(lax.psum(partial_grad, 'shot'), 'slab')  76.7 us
    scatter-add x3, other arithmetic, inject(): field.at[local_x, receivers[0, 1], receivers[0, 2]].add(values, mode='drop')  46.7 us
    psum x1, blocking collectives, body(): lax.psum(partial_grad, 'shot')  44.3 us
    ppermute x3, starting transfers between devices, extended(): lax.ppermute(lax.slice_in_dim(block, 0, width, axis=dim), axis, backward)  13.3 us
    ppermute x3, starting transfers between devices, extended(): lax.ppermute(lax.slice_in_dim(block, block.shape[dim] - width, None, axis...  8.3 us
    add x3, other arithmetic, body(): advanced = 2.0 * current - previous + courant * laplace(pad_sides(padded))  7.85 us
    ppermute x3, waiting for transfers between devices, extended(): lax.ppermute(lax.slice_in_dim(block, 0, width, axis=dim), axis, backward)  7.75 us
  transfers between devices with their start and end apart: 7, of which 4 were waited for; matrix products, arithmetic and copies ran while one was open for 1% of the time, Pallas kernels for 0%

profile of v1, /device:TPU:1, one launch (start us, length us, event | category | flops | bytes accessed | tf_op | source)
XLA Modules:
  0.0 354.7 jit_solution(237768908364594585)
XLA Ops:
  7.2 0.0 copy-start
  7.2 0.0 copy-start.4
  7.2 0.0 copy-start.3
  7.2 0.0 reduce-scatter.2.cloned.1.call-start
  7.2 1.1 slice_bitcast_fusion.1
  8.3 8.8 %collective-permute-start = (f32[4,64,128]{2,1,0:T(8,128)S(1)}, f32[4,64,128]{2,1,0:T(8,128)S(1)}, u32[]{:S(2)}, u32[]{:S(2)}) collective-permute-start(f32[4,64,128]{2,1,0:T(8,128)S(1)} %get-tuple-element.24), channel_id=1, source_target_pairs={{1,0},{2,1},{3,2},{4,3},{5,4},{6,5},{7,6},{8,7},{9,8},{10,9},{11,1... | collective-permute-start | bytes 393224 | tf_op jit(solution)/shard_map/ppermute | solution.py:19
  17.1 1.9 collective-permute-start.1
  19.0 0.7 fusion.67
  19.8 0.7 or_select_fusion
  20.5 0.0 collective-permute-done
  20.5 0.5 collective-permute-done.1
  21.0 1.6 select_maximum_fusion.4
  22.6 0.0 copy-done.4
  22.6 0.0 copy-done.3
  22.6 3.7 %fusion.13 = f32[16,64,128]{2,1,0:T(8,128)S(1)} fusion(f32[16,64,128]{2,1,0:T(8,128)S(1)} %copy-done.3, f32[16,64,128]{2,1,0:T(8,128)S(1)} %bitcast.63, f32[4,64,128]{2,1,0:T(8,128)} %collective-permute-done.1, f32[4,64,128]{2,1,0:T(8,128)S(1)} %collective-permute-done, f32[24,72,136]{2,1,0:T(8,128)S(1)} %select_maximum_fusion.4, f32[1,16,64,128]{3,2,1,0:T(8,128)} %param.10), kind=kLoop, calls=%fused_computation.40 | loop fusion | flops 5373952 | bytes 10747904 | tf_op jit(solution)/shard_map/add | solution.py:65
  26.2 15.6 %scatter_fusion = f32[16,64,128]{2,1,0:T(8,128)S(1)} fusion(f32[16,64,128]{2,1,0:T(8,128)S(1)} %fusion.13, s32[256]{0:T(256)S(1)} %bitcast.56, f32[256]{0:T(256)S(1)} %bitcast.69), kind=kCustom, calls=%fused_computation | custom fusion | flops 256 | bytes 6144 | tf_op jit(solution)/shard_map/scatter-add | solution.py:54
  41.8 4.5 %collective-permute-start.3 = (f32[4,64,128]{2,1,0:T(8,128)S(1)}, f32[4,64,128]{2,1,0:T(8,128)S(1)}, u32[]{:S(2)}, u32[]{:S(2)}) collective-permute-start(f32[4,64,128]{2,1,0:T(8,128)S(1)} %get-tuple-element.22), channel_id=1, source_target_pairs={{0,1},{1,2},{2,3},{3,4},{4,5},{5,6},{6,7},{7,8},{8,9},{9,10},{10,1... | collective-permute-start | bytes 393224 | tf_op jit(solution)/shard_map/ppermute | solution.py:16
  46.3 1.9 collective-permute-start.2
  48.2 0.0 collective-permute-done.3
  48.3 0.1 constant_dynamic-update-slice_fusion.1
  48.4 4.2 %collective-permute-done.2 = f32[4,64,128]{2,1,0:T(8,128)S(1)} collective-permute-done((f32[4,64,128]{2,1,0:T(8,128)S(1)}, f32[4,64,128]{2,1,0:T(8,128)S(1)}, u32[]{:S(2)}, u32[]{:S(2)}) %collective-permute-start.2) | collective-permute-done | bytes 131104 | tf_op jit(solution)/shard_map/ppermute | solution.py:19
  52.6 0.5 select_maximum_fusion.2
  53.1 2.1 fusion.46
  55.2 0.0 copy-start.6
  55.2 15.6 %scatter_fusion.1 = f32[16,64,128]{2,1,0:T(8,128)S(1)} fusion(f32[16,64,128]{2,1,0:T(8,128)S(1)} %fusion.46, s32[256]{0:T(256)S(1)} %bitcast.57, f32[256]{0:T(256)S(1)} %bitcast.68), kind=kCustom, calls=%fused_computation.1 | custom fusion | flops 256 | bytes 6144 | tf_op jit(solution)/shard_map/scatter-add | solution.py:54
  70.8 0.0 copy-start.1
  70.8 1.9 collective-permute-start.5
  72.8 0.0 copy-done.6
  72.8 0.6 fusion.68
  73.4 1.3 compare_and_fusion
  74.7 2.6 collective-permute-start.4
  77.3 0.0 collective-permute-done.5
  77.3 0.1 constant_dynamic-update-slice_fusion.5
  77.4 3.5 collective-permute-done.4
  81.0 0.5 select_maximum_fusion
  81.5 2.1 fusion.36
  83.6 15.6 %scatter_fusion.2 = f32[16,64,128]{2,1,0:T(8,128)S(1)} fusion(f32[16,64,128]{2,1,0:T(8,128)S(1)} %fusion.36, s32[256]{0:T(256)S(1)} %bitcast.58, f32[256]{0:T(256)S(1)} %bitcast.67), kind=kCustom, calls=%fused_computation.2 | custom fusion | flops 256 | bytes 6144 | tf_op jit(solution)/shard_map/scatter-add | solution.py:54
  99.2 0.0 copy-done.1
  99.2 0.0 copy-start.2
  99.2 0.0 copy-start.5
  99.2 1.6 fusion.58
  100.9 1.1 copy.23
  101.9 0.0 copy-done.2
  102.0 0.0 reduce-scatter.2.cloned.1.call-update
  102.0 0.0 copy-done.5
  102.0 0.2 reshape.127
  102.2 118.1 %reduce-scatter.2.cloned.1.call-done = f32[4,16,128]{2,1,0:T(8,128)} async-done(((f32[64,16,128]{2,1,0:T(8,128)}), f32[4,16,128]{2,1,0:T(8,128)}) %reduce-scatter.2.cloned.1.call-update) | async-done | bytes 32784 | tf_op jit(solution)/shard_map/reduce_scatter | solution.py:75
  220.3 2.8 reshape.124
  223.2 0.7 copy.24
  223.9 0.0 copy-done
  223.9 1.0 convolution_bitcast_fusion
  224.9 0.2 copy.31
  225.1 1.0 reshape.151
  226.1 0.3 convolution_bitcast_fusion.1
  226.4 44.3 %psum.14 = f32[64,8]{0,1:T(8,128)S(1)} all-reduce(f32[64,8]{0,1:T(8,128)S(1)} %convolution_bitcast_fusion.1), channel_id=1, replica_groups=mesh['shot'=16,'slab'=32] {'shot'}, use_global_device_ids=true, to_apply=%region_4.5 | all-reduce | flops 512 | bytes 4096 | tf_op jit(solution)/shard_map/psum | solution.py:93
  270.6 76.7 %psum.15 = f32[64,8]{0,1:T(8,128)S(1)} all-reduce(f32[64,8]{0,1:T(8,128)S(1)} %psum.14), channel_id=1, replica_groups=mesh['shot'=16,'slab'=32] {'slab'}, use_global_device_ids=true, to_apply=%region_5.6 | all-reduce | flops 512 | bytes 4096 | tf_op jit(solution)/shard_map/psum | solution.py:93
  347.3 0.6 broadcast_multiply_fusion
  (6 shorter events, 0.1 us)
Async XLA Ops:
  7.2 216.7 %copy-start = (f32[64,8]{0,1:T(8,128)S(1)}, f32[64,8]{0,1:T(8,128)}, u32[]{:S(2)}) copy-start(f32[64,8]{0,1:T(8,128)} %param.17) | copy-start | bytes 6148
  7.2 15.4 %copy-start.4 = (f32[1,16,64,128]{3,2,1,0:T(8,128)S(1)}, f32[1,16,64,128]{3,2,1,0:T(8,128)}, u32[]{:S(2)}) copy-start(f32[1,16,64,128]{3,2,1,0:T(8,128)} %param.9) | copy-start | bytes 1572868
  7.2 15.4 %copy-start.3 = (f32[16,64,128]{2,1,0:T(8,128)S(1)}, f32[16,64,128]{2,1,0:T(8,128)}, u32[]{:S(2)}) copy-start(f32[16,64,128]{2,1,0:T(8,128)} %param.11) | copy-start | bytes 1572868
  7.2 213.1 %reduce-scatter.2.cloned.1.call-start = ((), (), s32[]{:S(2)}) async-start(), calls=%async_computation.1 | async-start | bytes 557056 | tf_op jit(solution)/shard_map/reduce_scatter | solution.py:75
  8.3 12.2 %collective-permute-start = (f32[4,64,128]{2,1,0:T(8,128)S(1)}, f32[4,64,128]{2,1,0:T(8,128)S(1)}, u32[]{:S(2)}, u32[]{:S(2)}) collective-permute-start(f32[4,64,128]{2,1,0:T(8,128)S(1)} %get-tuple-element.24), channel_id=1, source_target_pairs={{1,0},{2,1},{3,2},{4,3},{5,4},{6,5},{7,6},{8,7},{9,8},{10,9},{11,1... | collective-permute-start | bytes 393224 | tf_op jit(solution)/shard_map/ppermute | solution.py:19
  17.1 3.9 %collective-permute-start.1 = (f32[4,64,128]{2,1,0:T(8,128)S(1)}, f32[4,64,128]{2,1,0:T(8,128)}, u32[]{:S(2)}, u32[]{:S(2)}) collective-permute-start(f32[4,64,128]{2,1,0:T(8,128)S(1)} %get-tuple-element.25), channel_id=1, source_target_pairs={{0,1},{1,2},{2,3},{3,4},{4,5},{5,6},{6,7},{7,8},{8,9},{9,10},{10,1... | collective-permute-start | bytes 393224 | tf_op jit(solution)/shard_map/ppermute | solution.py:16
  41.8 6.4 %collective-permute-start.3 = (f32[4,64,128]{2,1,0:T(8,128)S(1)}, f32[4,64,128]{2,1,0:T(8,128)S(1)}, u32[]{:S(2)}, u32[]{:S(2)}) collective-permute-start(f32[4,64,128]{2,1,0:T(8,128)S(1)} %get-tuple-element.22), channel_id=1, source_target_pairs={{0,1},{1,2},{2,3},{3,4},{4,5},{5,6},{6,7},{7,8},{8,9},{9,10},{10,1... | collective-permute-start | bytes 393224 | tf_op jit(solution)/shard_map/ppermute | solution.py:16
  46.3 6.3 %collective-permute-start.2 = (f32[4,64,128]{2,1,0:T(8,128)S(1)}, f32[4,64,128]{2,1,0:T(8,128)S(1)}, u32[]{:S(2)}, u32[]{:S(2)}) collective-permute-start(f32[4,64,128]{2,1,0:T(8,128)S(1)} %get-tuple-element.23), channel_id=1, source_target_pairs={{1,0},{2,1},{3,2},{4,3},{5,4},{6,5},{7,6},{8,7},{9,8},{10,9},{11,1... | collective-permute-start | bytes 393224 | tf_op jit(solution)/shard_map/ppermute | solution.py:19
  55.2 17.5 %copy-start.6 = (s32[1,2]{1,0:T(1,128)S(1)}, s32[1,2]{1,0:T(1,128)}, u32[]{:S(2)}) copy-start(s32[1,2]{1,0:T(1,128)} %param.15) | copy-start | bytes 28
  70.8 28.4 %copy-start.1 = (f32[16,64,128]{2,1,0:T(8,128)}, f32[16,64,128]{2,1,0:T(8,128)S(1)}, u32[]{:S(2)}) copy-start(f32[16,64,128]{2,1,0:T(8,128)S(1)} %scatter_fusion.1) | copy-start | bytes 1572868
  70.8 6.4 %collective-permute-start.5 = (f32[4,64,128]{2,1,0:T(8,128)S(1)}, f32[4,64,128]{2,1,0:T(8,128)S(1)}, u32[]{:S(2)}, u32[]{:S(2)}) collective-permute-start(f32[4,64,128]{2,1,0:T(8,128)S(1)} %get-tuple-element.18), channel_id=1, source_target_pairs={{0,1},{1,2},{2,3},{3,4},{4,5},{5,6},{6,7},{7,8},{8,9},{9,10},{10,1... | collective-permute-start | bytes 393224 | tf_op jit(solution)/shard_map/ppermute | solution.py:16
  74.7 6.3 %collective-permute-start.4 = (f32[4,64,128]{2,1,0:T(8,128)S(1)}, f32[4,64,128]{2,1,0:T(8,128)S(1)}, u32[]{:S(2)}, u32[]{:S(2)}) collective-permute-start(f32[4,64,128]{2,1,0:T(8,128)S(1)} %get-tuple-element.19), channel_id=1, source_target_pairs={{1,0},{2,1},{3,2},{4,3},{5,4},{6,5},{7,6},{8,7},{9,8},{10,9},{11,1... | collective-permute-start | bytes 393224 | tf_op jit(solution)/shard_map/ppermute | solution.py:19
  99.2 2.8 copy-start.2
  99.2 2.8 copy-start.5
Sparse Core Ops, SparseCore 0:
  102.1 118.1 reduce-scatter.1
